TPU v7x, 32 devices: a whole 2x2x4 slice. The times are simulated.
32 devices in a mesh: clip: 8 (over y, x, core), cap: 4 (over z).
Axes of the slice: x: 2, y: 2, z: 4, core: 2. Of those that a mesh axis runs over, the one named last changes fastest.
Arguments:
- teacher_audio: bfloat16 [6144, 512], P(('clip', 'cap')), may hold values from -2 to 2
- teacher_text: bfloat16 [6144, 512], P(('cap', 'clip')), may hold values from -2 to 2
- student_audio: bfloat16 [6144, 512], P(('clip', 'cap')), may hold values from -2 to 2
- student_text: bfloat16 [6144, 512], P(('cap', 'clip')), may hold values from -2 to 2
Outputs:
- audio_grad: float32 [6144, 512], P(('clip', 'cap'))
- text_grad: float32 [6144, 512], P(('cap', 'clip'))
All inputs are finite; a program needn't handle non-finite values.
Results may differ from a plain program's by a relative error of at most 0.0026.
Values may be sent and summed in bfloat16 or wider, within the bound.
A program may use at most 128 MiB of HBM per device.

v0:
```python
import jax
import jax.numpy as jnp
from jax import lax
from jax.sharding import PartitionSpec as P

ITERS = 3


def contract_rows(left_mat, right_mat):
    return lax.dot_general(
        left_mat, right_mat, (((1,), (1,)), ((), ())), preferred_element_type=jnp.float32
    )


def contract_first(left_mat, right_mat):
    return lax.dot_general(
        left_mat, right_mat, (((0,), (0,)), ((), ())), preferred_element_type=jnp.float32
    )


def body(teacher_audio, teacher_text, student_audio, student_text):
    audio_teacher, audio_student = (
        lax.all_gather(teacher_audio, "cap", axis=0, tiled=True),
        lax.all_gather(student_audio, "cap", axis=0, tiled=True),
    )
    text_teacher, text_student = (
        lax.all_gather(teacher_text, "clip", axis=0, tiled=True),
        lax.all_gather(student_text, "clip", axis=0, tiled=True),
    )
    teacher_logits = 10.0 * contract_rows(audio_teacher, text_teacher)
    student_logits = 10.0 * contract_rows(audio_student, text_student)
    teacher_max, student_max = lax.pmax(
        (jnp.max(teacher_logits, axis=1), jnp.max(student_logits, axis=1)), "cap"
    )
    student_exp = jnp.exp(student_logits - student_max[:, None])
    student_total = lax.psum(jnp.sum(student_exp, axis=1), "cap")
    kernel = jnp.exp(teacher_logits - teacher_max[:, None])
    weights_row = jnp.ones((kernel.shape[0],), jnp.float32)
    column_scale = jnp.ones((kernel.shape[1],), jnp.float32)
    for sweep_index in range(ITERS):
        column = lax.psum(jnp.dot(weights_row, kernel, precision=lax.Precision.HIGHEST), "clip")
        column_scale = 1.0 / column
        row_total = lax.psum(jnp.dot(kernel, column_scale, precision=lax.Precision.HIGHEST), "cap")
        weights_row = 1.0 / row_total
    target = weights_row[:, None] * kernel * column_scale[None, :]
    student_prob = student_exp / student_total[:, None]
    residual = (student_prob - target).astype(jnp.bfloat16)
    audio_grad = lax.psum_scatter(
        10.0 * jnp.dot(residual, text_student, preferred_element_type=jnp.float32),
        "cap",
        scatter_dimension=0,
        tiled=True,
    )
    text_grad = lax.psum_scatter(
        10.0 * contract_first(residual, audio_student), "clip", scatter_dimension=0, tiled=True
    )
    return (audio_grad, text_grad)


def solution(mesh):
    placed = (
        P(("clip", "cap"), None),
        P(("cap", "clip"), None),
        P(("clip", "cap"), None),
        P(("cap", "clip"), None),
    )
    return jax.shard_map(
        body,
        mesh=mesh,
        in_specs=placed,
        out_specs=(P(("clip", "cap"), None), P(("cap", "clip"), None)),
        check_vma=False,
    )
```

profile of v0, /device:TPU:0, one launch (start us, length us, event | category | flops | bytes accessed | tf_op | source)
XLA Modules:
  0.0 283.5 jit_solution(820184726141326755)
XLA Ops:
  7.2 0.0 all-gather.5.cloned.1.call-start
  7.2 0.7 all-gather.5.cloned.1.call-update
  7.9 0.0 all-gather.3.cloned.1.call-start
  7.9 0.7 all-gather.3.cloned.1.call-update
  8.6 0.0 reduce-scatter.3.cloned.1.call-start
  8.7 21.5 %all_gather.12 = bf16[768,512]{1,0:T(8,128)(2,1)S(1)} all-gather(bf16[192,512]{1,0:T(8,128)(2,1)} %param.6), channel_id=1, replica_groups=mesh['clip'=8,'cap'=4] {'cap'}, dimensions={0}, use_global_device_ids=true | all-gather | bytes 983040 | tf_op jit(solution)/shard_map/all_gather | solution.py:24
  30.2 17.9 %all_gather.14 = bf16[768,512]{1,0:T(8,128)(2,1)S(1)} all-gather(bf16[192,512]{1,0:T(8,128)(2,1)} %param.4), channel_id=1, replica_groups=mesh['clip'=8,'cap'=4] {'cap'}, dimensions={0}, use_global_device_ids=true | all-gather | bytes 983040 | tf_op jit(solution)/shard_map/all_gather | solution.py:23
  48.1 5.0 %multiply_reduce_fusion = (f32[768]{0:T(1024)S(1)}, f32[768,1536]{1,0:T(8,128)}) fusion(bf16[768,512]{1,0:T(8,128)(2,1)S(1)} %all_gather.14, bf16[1536,512]{1,0:T(8,128)(2,1)} %all-gather.5.cloned.1.call-done), kind=kOutput, calls=%fused_computation.3 | convolution fusion | flops 1210318080 | bytes 7080960 | tf_op jit(solution)/shard_map/dot_general | solution.py:10
  53.1 12.6 %all-gather.3.cloned.1.call-done = bf16[1536,512]{1,0:T(8,128)(2,1)} async-done(((bf16[192,512]{1,0:T(8,128)(2,1)}), bf16[1536,512]{1,0:T(8,128)(2,1)}) %all-gather.3.cloned.1.call-update) | async-done | bytes 1572880 | tf_op jit(solution)/shard_map/all_gather | solution.py:28
  65.7 5.0 %multiply_reduce_fusion.1 = (f32[768]{0:T(1024)S(1)}, f32[768,1536]{1,0:T(8,128)}) fusion(bf16[768,512]{1,0:T(8,128)(2,1)S(1)} %all_gather.12, bf16[1536,512]{1,0:T(8,128)(2,1)} %all-gather.3.cloned.1.call-done), kind=kOutput, calls=%fused_computation.4 | convolution fusion | flops 1210318080 | bytes 7080960 | tf_op jit(solution)/shard_map/dot_general | solution.py:10
  70.7 11.8 %all-reduce.1 = (f32[768]{0:T(1024)S(1)}, f32[768]{0:T(1024)S(1)}) all-reduce(f32[768]{0:T(1024)S(1)} %get-tuple-element.6, f32[768]{0:T(1024)S(1)} %get-tuple-element.8), channel_id=1, replica_groups=mesh['clip'=8,'cap'=4] {'cap'}, use_global_device_ids=true, to_apply=%region_5.0 | all-reduce | flops 1536 | bytes 12288 | tf_op jit(solution)/shard_map/pmax | solution.py:32
  82.5 5.3 %convolution_reduce_fusion.2 = f32[1536]{0:T(1024)S(1)} fusion(f32[768,1536]{1,0:T(8,128)} %get-tuple-element.7, f32[768]{0:T(1024)S(1)} %get-tuple-element.4), kind=kOutput, calls=%fused_computation.10 | convolution fusion | flops 16515072 | bytes 4727808 | tf_op jit(solution)/shard_map/dot_general | solution.py:41
  87.8 12.1 %psum.50 = f32[1536]{0:T(1024)S(1)} all-reduce(f32[1536]{0:T(1024)S(1)} %convolution_reduce_fusion.2), channel_id=1, replica_groups=mesh['clip'=8,'cap'=4] {'clip'}, use_global_device_ids=true, to_apply=%region_6.0 | all-reduce | flops 1536 | bytes 12288 | tf_op jit(solution)/shard_map/psum | solution.py:41
  99.9 6.9 %convolution_reduce_fusion.5 = f32[768]{0:T(1024)S(1)} fusion(f32[1536,1]{0,1:T(1,128)S(1)} %reshape.11, f32[768,1536]{1,0:T(8,128)} %get-tuple-element.7, f32[768]{0:T(1024)S(1)} %get-tuple-element.4), kind=kOutput, calls=%fused_computation.13 | convolution fusion | flops 16515072 | bytes 4730880 | tf_op jit(solution)/shard_map/dot_general | solution.py:43
  106.8 8.4 %psum.51 = f32[768]{0:T(1024)S(1)} all-reduce(f32[768]{0:T(1024)S(1)} %convolution_reduce_fusion.5), channel_id=1, replica_groups=mesh['clip'=8,'cap'=4] {'cap'}, use_global_device_ids=true, to_apply=%region_7.0 | all-reduce | flops 768 | bytes 6144 | tf_op jit(solution)/shard_map/psum | solution.py:43
  115.2 5.3 %convolution_reduce_fusion.1 = f32[1536]{0:T(1024)S(1)} fusion(f32[768,1]{0,1:T(1,128)S(1)} %reshape.13, f32[768,1536]{1,0:T(8,128)} %get-tuple-element.7, f32[768]{0:T(1024)S(1)} %get-tuple-element.4), kind=kOutput, calls=%fused_computation.9 | convolution fusion | flops 16515072 | bytes 4730880 | tf_op jit(solution)/shard_map/dot_general | solution.py:41
  120.5 12.0 %psum.52 = f32[1536]{0:T(1024)S(1)} all-reduce(f32[1536]{0:T(1024)S(1)} %convolution_reduce_fusion.1), channel_id=1, replica_groups=mesh['clip'=8,'cap'=4] {'clip'}, use_global_device_ids=true, to_apply=%region_8.0 | all-reduce | flops 1536 | bytes 12288 | tf_op jit(solution)/shard_map/psum | solution.py:41
  132.6 6.9 %convolution_reduce_fusion.4 = f32[768]{0:T(1024)S(1)} fusion(f32[1536,1]{0,1:T(1,128)S(1)} %reshape.15, f32[768,1536]{1,0:T(8,128)} %get-tuple-element.7, f32[768]{0:T(1024)S(1)} %get-tuple-element.4), kind=kOutput, calls=%fused_computation.12 | convolution fusion | flops 16515072 | bytes 4730880 | tf_op jit(solution)/shard_map/dot_general | solution.py:43
  139.5 10.4 %psum.53 = f32[768]{0:T(1024)S(1)} all-reduce(f32[768]{0:T(1024)S(1)} %convolution_reduce_fusion.4), channel_id=1, replica_groups=mesh['clip'=8,'cap'=4] {'cap'}, use_global_device_ids=true, to_apply=%region_9.0 | all-reduce | flops 768 | bytes 6144 | tf_op jit(solution)/shard_map/psum | solution.py:43
  149.9 5.3 %convolution_reduce_fusion = f32[1536]{0:T(1024)S(1)} fusion(f32[768,1]{0,1:T(1,128)S(1)} %reshape.17, f32[768,1536]{1,0:T(8,128)} %get-tuple-element.7, f32[768]{0:T(1024)S(1)} %get-tuple-element.4), kind=kOutput, calls=%fused_computation.8 | convolution fusion | flops 16515072 | bytes 4730880 | tf_op jit(solution)/shard_map/dot_general | solution.py:41
  155.2 12.3 %psum.54 = f32[1536]{0:T(1024)S(1)} all-reduce(f32[1536]{0:T(1024)S(1)} %convolution_reduce_fusion), channel_id=1, replica_groups=mesh['clip'=8,'cap'=4] {'clip'}, use_global_device_ids=true, to_apply=%region_10.0 | all-reduce | flops 1536 | bytes 12288 | tf_op jit(solution)/shard_map/psum | solution.py:41
  167.5 6.9 %convolution_reduce_fusion.3 = f32[768]{0:T(1024)S(1)} fusion(f32[1536,1]{0,1:T(1,128)S(1)} %reshape.19, f32[768,1536]{1,0:T(8,128)} %get-tuple-element.7, f32[768]{0:T(1024)S(1)} %get-tuple-element.4), kind=kOutput, calls=%fused_computation.11 | convolution fusion | flops 16515072 | bytes 4730880 | tf_op jit(solution)/shard_map/dot_general | solution.py:43
  174.4 3.2 %fusion = f32[768]{0:T(1024)S(1)} fusion(f32[768,1536]{1,0:T(8,128)} %get-tuple-element.9, f32[768]{0:T(1024)S(1)} %get-tuple-element.5), kind=kLoop, calls=%fused_computation.5 | loop fusion | flops 3538176 | bytes 4724736 | tf_op jit(solution)/shard_map/reduce_sum | solution.py:36
  177.7 8.5 %all-reduce = (f32[768]{0:T(1024)S(1)}, f32[768]{0:T(1024)S(1)}) all-reduce(f32[768]{0:T(1024)S(1)} %convolution_reduce_fusion.3, f32[768]{0:T(1024)S(1)} %fusion), channel_id=1, replica_groups=mesh['clip'=8,'cap'=4] {'cap'}, use_global_device_ids=true, to_apply=%region_11.0 | all-reduce | flops 1536 | bytes 12288 | tf_op jit(solution)/shard_map/psum | solution.py:43
  186.2 4.9 %subtract_convert_fusion = bf16[768,1536]{1,0:T(8,128)(2,1)S(1)} fusion(f32[768,1536]{1,0:T(8,128)} %get-tuple-element.9, f32[1536]{0:T(1024)S(1)} %broadcast_divide_fusion, f32[768]{0:T(1024)S(1)} %broadcast_divide_fusion.5, f32[768]{0:T(1024)S(1)} %get-tuple-element.3, f32[768]{0:T(1024)S(1)} %get-tuple-element.5, f32[768]{0:T(1024)S(1)} %get-tuple-element.4, ...), kind=kLoop, calls=%fused_computation | loop fusion | flops 10616832 | bytes 11814912 | tf_op jit(solution)/shard_map/convert_element_type | solution.py:47
  191.2 2.5 convolution_multiply_fusion.1
  193.7 0.0 reduce-scatter.3.cloned.1.call-update
  193.7 0.0 reduce-scatter.5.cloned.1.call-start
  193.8 3.1 %convolution_multiply_fusion = f32[1536,512]{1,0:T(8,128)} fusion(bf16[768,1536]{1,0:T(8,128)(2,1)S(1)} %subtract_convert_fusion, bf16[768,512]{1,0:T(8,128)(2,1)S(1)} %all_gather.12), kind=kOutput, calls=%fused_computation.6 | convolution fusion | flops 1208745984 | bytes 6291456 | tf_op jit(solution)/shard_map/dot_general | solution.py:16
  196.9 0.0 reduce-scatter.5.cloned.1.call-update
  196.9 31.3 %reduce-scatter.3.cloned.1.call-done = f32[192,512]{1,0:T(8,128)} async-done(((f32[768,512]{1,0:T(8,128)}), f32[192,512]{1,0:T(8,128)}) %reduce-scatter.3.cloned.1.call-update) | async-done | bytes 393232 | tf_op jit(solution)/shard_map/reduce_scatter | solution.py:48
  228.2 48.7 %reduce-scatter.5.cloned.1.call-done = f32[192,512]{1,0:T(8,128)} async-done(((f32[1536,512]{1,0:T(8,128)}), f32[192,512]{1,0:T(8,128)}) %reduce-scatter.5.cloned.1.call-update) | async-done | bytes 393232 | tf_op jit(solution)/shard_map/reduce_scatter | solution.py:54
  (14 shorter events, 0.1 us)
Async XLA Ops:
  7.2 41.0 %all-gather.5.cloned.1.call-start = ((), (), s32[]{:S(2)}) async-start(), calls=%async_computation.3 | async-start | bytes 1769472 | tf_op jit(solution)/shard_map/all_gather | solution.py:27
  7.9 57.8 %all-gather.3.cloned.1.call-start = ((), (), s32[]{:S(2)}) async-start(), calls=%async_computation.2 | async-start | bytes 1769472 | tf_op jit(solution)/shard_map/all_gather | solution.py:28
  8.6 219.5 %reduce-scatter.3.cloned.1.call-start = ((), (), s32[]{:S(2)}) async-start(), calls=%async_computation.4 | async-start | bytes 1966080 | tf_op jit(solution)/shard_map/reduce_scatter | solution.py:48
  186.2 5.0 %copy-start = (bf16[1536,512]{1,0:T(8,128)(2,1)S(1)}, bf16[1536,512]{1,0:T(8,128)(2,1)}, u32[]{:S(2)}) copy-start(bf16[1536,512]{1,0:T(8,128)(2,1)} %all-gather.3.cloned.1.call-done) | copy-start | bytes 4718596
  193.7 83.2 %reduce-scatter.5.cloned.1.call-start = ((), (), s32[]{:S(2)}) async-start(), calls=%async_computation.5 | async-start | bytes 3538944 | tf_op jit(solution)/shard_map/reduce_scatter | solution.py:54
Sparse Core Ops, SparseCore 0:
  9.8 28.2 all-gather.4
  40.1 25.5 all-gather.2
  193.9 34.2 reduce-scatter.2
  232.0 44.8 reduce-scatter.4
where the time goes:
time: 284 us; the launch traced here: 283 us
  blocking collectives  115 us (40%)
  waiting for transfers between devices  94 us (33%)
  matrix products  52.1 us (18%)
  between operations  13.9 us (5%)
  other arithmetic  8.21 us (3%)
    reduce_scatter x1, waiting for transfers between devices, body(): lax.psum_scatter(10.0 * contract_first(residual, audio_student), 'clip',...  48.7 us
    psum x3, blocking collectives, body(): lax.psum(jnp.dot(weights_row, kernel, precision=lax.Precision.HIGHEST), '...  36.4 us
    reduce_scatter x1, waiting for transfers between devices, body(): lax.psum_scatter(10.0 * jnp.dot(residual, text_student, preferred_element...  31.3 us
    psum x3, blocking collectives, body(): lax.psum(jnp.dot(kernel, column_scale, precision=lax.Precision.HIGHEST),...  27.3 us
    all_gather x1, blocking collectives, body(): lax.all_gather(student_audio, 'cap', axis=0, tiled=True)  21.5 us
    dot_general x3, matrix products, body(): jnp.dot(kernel, column_scale, precision=lax.Precision.HIGHEST)  20.8 us
    all_gather x1, blocking collectives, body(): lax.all_gather(teacher_audio, 'cap', axis=0, tiled=True)  17.9 us
    dot_general x3, matrix products, body(): jnp.dot(weights_row, kernel, precision=lax.Precision.HIGHEST)  15.8 us
  transfers between devices with their start and end apart: 4, of which 3 were waited for; matrix products, arithmetic and copies ran while one was open for 3% of the time, Pallas kernels for 0%

commit v1 on v0

v1 whole, which is shorter than its diff:
```python
import functools

import jax
import jax.numpy as jnp
from jax import lax
from jax.experimental import pallas as pl
from jax.experimental.pallas import tpu as pltpu
from jax.sharding import PartitionSpec as P

ITERS = 3
LANE = 128
MESH = pl.DeviceIdType.MESH


def flip(index, bit):
    return index + bit * (1 - 2 * ((index // bit) % 2))


def flip_mask(index, mask, count):
    bit = 1
    while bit < count:
        if mask & bit:
            index = flip(index, bit)
        bit *= 2
    return index


def tree_orders(count):
    bits = []
    bit = 2
    while bit < count:
        bits.append(bit)
        bit *= 2
    tail = [1] if count > 1 else []
    return (bits + tail, bits[::-1] + tail)


def children(mask, order):
    last = -1
    for position, bit in enumerate(order):
        if mask & bit:
            last = position
    return [bit for bit in order[last + 1:]]


def mask_sequence(count, order):
    out, level = [], [0]
    while level:
        following = []
        for mask in level:
            for bit in children(mask, order):
                following.append(mask | bit)
        out.extend(following)
        level = following
    return out


def kernel(
    nclip, ncap, shard,
    ta_ref, tt_ref, sa_ref, st_ref, ag_ref, tg_ref,
    abuf, tbuf, kmat, smat, rmat, lbuf, pbuf, wrep, srep, crep, mrep, smax, ssum,
    rowx, colx, maxx, lastx, asend, arecv, tsend, trecv,
    az_send, az_recv, tx_send, tx_recv, rx_send, rx_recv, cx_send, cx_recv,
    as_send, as_recv, ts_send, ts_recv,
):
    clip = lax.axis_index("clip")
    cap = lax.axis_index("cap")
    rows, cols, width = shard * ncap, shard * nclip, ta_ref.shape[1]
    tiles = cols // LANE
    orders = tree_orders(nclip)
    if smat.shape != kmat.shape:
        smat = rmat

    def remote(src, dst, ss, rs, to_clip, to_cap):
        return pltpu.make_async_remote_copy(
            src_ref=src, dst_ref=dst, send_sem=ss, recv_sem=rs,
            device_id=(to_clip, to_cap), device_id_type=MESH)

    barrier = pltpu.get_barrier_semaphore()
    for j in range(1, ncap):
        pl.semaphore_signal(barrier, inc=1, device_id=(clip, lax.rem(cap + j, ncap)), device_id_type=MESH)
    for j in range(1, nclip):
        pl.semaphore_signal(barrier, inc=1, device_id=(lax.rem(clip + j, nclip), cap), device_id_type=MESH)

    for t, (a, x) in enumerate(((ta_ref, tt_ref), (sa_ref, st_ref))):
        abuf[t, cap] = a[...]
        tbuf[t, clip] = x[...]
    pl.semaphore_wait(barrier, ncap + nclip - 2)

    own_audio, own_text = (ta_ref, sa_ref), (tt_ref, st_ref)

    def tree_copy(t, mask, bit):
        src_index = flip_mask(clip, mask, nclip)
        src = own_text[t] if mask == 0 else tbuf.at[t, src_index]
        return remote(src, tbuf.at[t, src_index], tx_send.at[t, mask | bit],
                      tx_recv.at[t, mask | bit], flip(clip, bit), cap)

    def tree_forward(t, mask):
        for bit in children(mask, orders[t]):
            tree_copy(t, mask, bit).start()

    def tree_wait(t, mask):
        landed = tbuf.at[t, flip_mask(clip, mask, nclip)]
        remote(landed, landed, tx_send.at[t, mask], tx_recv.at[t, mask], clip, cap).wait_recv()

    def line_copy(t, s, step, own):
        src = own_audio[t] if own else abuf.at[t, s]
        side = 0 if step < 0 else 1
        return remote(src, abuf.at[t, s], az_send.at[t, side, s], az_recv.at[t, s], clip, cap + step)

    def line_own(t):
        @pl.when(cap + 1 < ncap)
        def _():
            line_copy(t, cap, 1, True).start()

        @pl.when(cap >= 1)
        def _():
            line_copy(t, cap, -1, True).start()

    def line_left(t, d):
        s = cap - d
        line_copy(t, s, 1, False).wait_recv()

        @pl.when(cap + 1 < ncap)
        def _():
            line_copy(t, s, 1, False).start()

    def line_right(t, d):
        s = cap + d
        line_copy(t, s, -1, False).wait_recv()

        @pl.when(cap >= 1)
        def _():
            line_copy(t, s, -1, False).start()

    def line_step(t, d):
        @pl.when(cap >= d)
        def _():
            line_left(t, d)

        @pl.when(cap + d < ncap)
        def _():
            line_right(t, d)

    step_cols = 512 if cols % 512 == 0 else LANE

    def logits(t, s):
        rs = pl.ds(pl.multiple_of(s * shard, shard), shard)
        a = abuf[t, s]
        text = tbuf.at[t].reshape(cols, width)
        top = None
        for j in range(0, cols, step_cols):
            part = 10.0 * lax.dot_general(
                a, text[j:j + step_cols, :], (((1,), (1,)), ((), ())),
                preferred_element_type=jnp.float32)
            lbuf[:, j:j + step_cols] = part
            here = jnp.max(part, axis=1, keepdims=True)
            top = here if top is None else jnp.maximum(top, here)
        total = None
        for j in range(0, cols, step_cols):
            value = jnp.exp(lbuf[:, j:j + step_cols] - top)
            if t == 0:
                kmat[rs, j:j + step_cols] = value
            else:
                smat[rs, j:j + step_cols] = value.astype(smat.dtype)
                here = jnp.sum(value, axis=1, keepdims=True)
                total = here if total is None else total + here
        wide = jnp.broadcast_to(top, (shard, LANE))
        if t == 0:
            mrep[rs, :] = wide
        else:
            smax[rs, :] = wide
            ssum[rs, :] = jnp.broadcast_to(total, (shard, LANE))

    tree_forward(0, 0)
    line_own(0)
    sequence = mask_sequence(nclip, orders[0])
    waited = 0
    for d in range(1, ncap - 1):
        amount = len(sequence) if d == ncap - 2 else min(len(sequence), waited + nclip // 2)
        if d == 1:
            line_step(0, 1)
        for mask in sequence[waited:amount]:
            tree_wait(0, mask)
            tree_forward(0, mask)
        waited = amount
        if d > 1:
            line_step(0, d)
    for mask in sequence[waited:]:
        tree_wait(0, mask)
        tree_forward(0, mask)
    tree_forward(1, 0)
    line_own(1)
    logits(0, cap)

    def early(t, d):
        @pl.when(cap >= d)
        def _():
            logits(t, cap - d)

        @pl.when(cap + d < ncap)
        def _():
            logits(t, cap + d)

    def early_loop(t, first, last):
        def one(d, carry):
            early(t, d)
            return carry
        lax.fori_loop(first, last, one, 0)

    if ncap > 1:
        def one_teacher(d, carry):
            @pl.when(d == ncap - 1)
            def _():
                if ncap > 2:
                    line_step(0, ncap - 1)
                else:
                    line_step(0, 1)
            early(0, d)
            return carry
        lax.fori_loop(1, ncap, one_teacher, 0)

    def spread(buffer, sends, recvs, k, along_cap):
        count, me = (ncap, cap) if along_cap else (nclip, clip)
        for j in range(1, count):
            peer = lax.rem(me + j, count)
            remote(buffer.at[0], buffer.at[j], sends.at[k, j], recvs.at[k, j],
                   clip if along_cap else peer, peer if along_cap else cap).start()

    def gathered(buffer, sends, recvs, k, along_cap):
        count = ncap if along_cap else nclip
        for j in range(1, count):
            copy = remote(buffer.at[0], buffer.at[j], sends.at[k, j], recvs.at[k, j], clip, cap)
            copy.wait_recv()
            copy.wait_send()

    def across(ref):
        return ref[...].T[0:1, :]

    def down(vector):
        return jnp.broadcast_to(vector, (LANE, rows)).T

    block = 64

    def column_pass():
        def one(i, carry):
            rs = pl.ds(pl.multiple_of(i * block, block), block)
            w = wrep[rs, :]
            out = []
            for t in range(tiles):
                product = kmat[rs, t * LANE:(t + 1) * LANE] * w
                out.append(carry[t] + jnp.sum(product.reshape(block // 8, 8, LANE), axis=0))
            return tuple(out)
        acc = lax.fori_loop(0, rows // block, one, tuple(jnp.zeros((8, LANE), jnp.float32) for _ in range(tiles)))
        return [jnp.sum(a, axis=0, keepdims=True) for a in acc]

    def row_pass():
        def one(i, carry):
            rs = pl.ds(pl.multiple_of(i * block, block), block)
            acc = jnp.zeros((block // 8, 8, LANE), jnp.float32)
            for t in range(tiles):
                acc = acc + kmat[rs, t * LANE:(t + 1) * LANE].reshape(block // 8, 8, LANE) * crep[:, t * LANE:(t + 1) * LANE][None]
            pbuf[rs, :] = acc.reshape(block, LANE)
            return carry
        lax.fori_loop(0, rows // block, one, 0)
        return jnp.sum(pbuf[...].T, axis=0, keepdims=True)

    student_sequence = mask_sequence(nclip, orders[1])
    half = nclip // 2

    def student_trees(masks):
        for mask in masks:
            tree_wait(1, mask)
            tree_forward(1, mask)

    def fill_max():
        student_trees(student_sequence[:half])
        if ncap > 1:
            line_step(1, 1)

    def fill_column_0():
        student_trees(student_sequence[half:])
        for d in range(2, ncap - 1):
            line_step(1, d)

    def fill_row_0():
        if ncap > 2:
            line_step(1, ncap - 1)
        logits(1, cap)

    cuts = [1, 1 + (ncap - 1) // 3, 1 + 2 * (ncap - 1) // 3, ncap]

    fills = {
        ("c", 0): fill_column_0,
        ("r", 0): fill_row_0,
        ("c", 1): lambda: early_loop(1, cuts[0], cuts[1]),
        ("r", 1): lambda: early_loop(1, cuts[1], cuts[2]),
        ("c", 2): lambda: early_loop(1, cuts[2], cuts[3]),
    }

    local_max = across(mrep)
    maxx[0] = local_max
    spread(maxx, rx_send, rx_recv, 0, True)
    fill_max()
    gathered(maxx, rx_send, rx_recv, 0, True)
    top = maxx[0]
    for j in range(1, ncap):
        top = jnp.maximum(top, maxx[j])
    factor = jnp.exp(maxx[0] - top)
    wrep[...] = down(factor)

    for it in range(ITERS):
        for t, part in enumerate(column_pass()):
            colx[it, 0, :, t * LANE:(t + 1) * LANE] = part
        spread(colx.at[it], cx_send, cx_recv, it, False)
        fills[("c", it)]()
        gathered(colx.at[it], cx_send, cx_recv, it, False)
        column = colx[it, 0]
        for j in range(1, nclip):
            column = column + colx[it, j]
        crep[...] = jnp.broadcast_to(1.0 / column, (8, cols))
        row = row_pass() * factor
        if it < ITERS - 1:
            rowx[it, 0] = row
            spread(rowx.at[it], rx_send, rx_recv, it + 1, True)
            fills[("r", it)]()
            gathered(rowx.at[it], rx_send, rx_recv, it + 1, True)
            total = rowx[it, 0]
            for j in range(1, ncap):
                total = total + rowx[it, j]
        else:
            lastx[0, 0:1, :] = row
            lastx[0, 1:2, :] = across(smax)
            lastx[0, 2:3, :] = across(ssum)
            spread(lastx, rx_send, rx_recv, it + 1, True)
            gathered(lastx, rx_send, rx_recv, it + 1, True)
            total = lastx[0, 0:1, :]
            best = lastx[0, 1:2, :]
            for j in range(1, ncap):
                total = total + lastx[j, 0:1, :]
                best = jnp.maximum(best, lastx[j, 1:2, :])
            own = jnp.exp(lastx[0, 1:2, :] - best)
            norm = own * lastx[0, 2:3, :]
            for j in range(1, ncap):
                norm = norm + jnp.exp(lastx[j, 1:2, :] - best) * lastx[j, 2:3, :]
            srep[...] = down(own / norm)
        wrep[...] = down(factor / total)

    text_student = tbuf.at[1].reshape(cols, width)

    def audio_part(i, carry):
        s = lax.rem(cap + 1 + i, ncap)
        rs = pl.ds(pl.multiple_of(s * shard, shard), shard)
        w, p = wrep[rs, :], srep[rs, :]
        for t in range(tiles):
            cs = slice(t * LANE, (t + 1) * LANE)
            target = (w * kmat[rs, cs]) * crep[0:1, cs]
            rmat[rs, cs] = (smat[rs, cs].astype(jnp.float32) * p - target).astype(jnp.bfloat16)
        grad = 10.0 * jnp.dot(rmat[rs, :], text_student[...], preferred_element_type=jnp.float32)

        @pl.when(i < ncap - 1)
        def _():
            asend[s] = grad.astype(jnp.bfloat16)
            remote(asend.at[s], arecv.at[i + 1], as_send.at[i + 1], as_recv.at[i + 1], clip, s).start()

        @pl.when(i == ncap - 1)
        def _():
            ag_ref[...] = grad
        return carry

    lax.fori_loop(0, ncap, audio_part, 0)

    group = 2 if nclip % 2 == 0 else nclip
    groups = nclip // group
    audio_student = abuf.at[1].reshape(rows, width)

    def text_part(i, carry):
        q = lax.rem(clip // group + 1 + i, groups)
        cs = pl.ds(pl.multiple_of(q * (group * shard), LANE), group * shard)
        grad = 10.0 * lax.dot_general(
            rmat[:, cs], audio_student[...], (((0,), (0,)), ((), ())),
            preferred_element_type=jnp.float32)
        for g in range(group):
            dest = q * group + g

            @pl.when(dest == clip)
            def _():
                tg_ref[...] = grad[g * shard:(g + 1) * shard, :]

            @pl.when(dest != clip)
            def _():
                offset = lax.rem(dest - clip + nclip, nclip)
                tsend[dest] = grad[g * shard:(g + 1) * shard, :].astype(jnp.bfloat16)
                remote(tsend.at[dest], trecv.at[offset], ts_send.at[offset], ts_recv.at[offset], dest, cap).start()
        return carry

    lax.fori_loop(0, groups, text_part, 0)

    for t in range(2):
        for mask in range(1, nclip):
            bit = mask & -mask
            for cand in orders[t]:
                if mask & cand:
                    bit = cand
            tree_copy(t, mask ^ bit, bit).wait_send()

        def drain(s, carry, t=t):
            @pl.when(jnp.logical_and(s <= cap, cap + 1 < ncap))
            def _():
                line_copy(t, s, 1, False).wait_send()

            @pl.when(jnp.logical_and(s >= cap, cap >= 1))
            def _():
                line_copy(t, s, -1, False).wait_send()
            return carry
        lax.fori_loop(0, ncap, drain, 0)

    for j in range(1, ncap):
        copy = remote(asend.at[0], arecv.at[j], as_send.at[j], as_recv.at[j], clip, cap)
        copy.wait_recv()
        copy.wait_send()
    total = ag_ref[...]
    for j in range(1, ncap):
        total = total + arecv[j].astype(jnp.float32)
    ag_ref[...] = total
    for j in range(1, nclip):
        copy = remote(tsend.at[0], trecv.at[j], ts_send.at[j], ts_recv.at[j], clip, cap)
        copy.wait_recv()
        copy.wait_send()
    total = tg_ref[...]
    for j in range(1, nclip):
        total = total + trecv[j].astype(jnp.float32)
    tg_ref[...] = total


def body(nclip, ncap, teacher_audio, teacher_text, student_audio, student_text):
    shard, width = teacher_audio.shape
    rows, cols = shard * ncap, shard * nclip
    f32, bf16 = jnp.float32, jnp.bfloat16
    roomy = rows * cols <= 2 ** 21
    dma = pltpu.SemaphoreType.DMA
    return pl.pallas_call(
        functools.partial(kernel, nclip, ncap, shard),
        out_shape=(jax.ShapeDtypeStruct((shard, width), f32),) * 2,
        in_specs=[pl.BlockSpec(memory_space=pltpu.VMEM)] * 4,
        out_specs=(pl.BlockSpec(memory_space=pltpu.VMEM),) * 2,
        scratch_shapes=[
            pltpu.VMEM((2, ncap, shard, width), bf16),
            pltpu.VMEM((2, nclip, shard, width), bf16),
            pltpu.VMEM((rows, cols), f32),
            pltpu.VMEM((rows, cols) if roomy else (8, LANE), f32),
            pltpu.VMEM((rows, cols), bf16),
            pltpu.VMEM((shard, cols), f32),
            pltpu.VMEM((rows, LANE), f32),
            pltpu.VMEM((rows, LANE), f32),
            pltpu.VMEM((rows, LANE), f32),
            pltpu.VMEM((8, cols), f32),
            pltpu.VMEM((rows, LANE), f32),
            pltpu.VMEM((rows, LANE), f32),
            pltpu.VMEM((rows, LANE), f32),
            pltpu.VMEM((ITERS, ncap, 1, rows), f32),
            pltpu.VMEM((ITERS, nclip, 1, cols), f32),
            pltpu.VMEM((ncap, 1, rows), f32),
            pltpu.VMEM((ncap, 3, rows), f32),
            pltpu.VMEM((ncap, shard, width), bf16),
            pltpu.VMEM((ncap, shard, width), bf16),
            pltpu.VMEM((nclip, shard, width), bf16),
            pltpu.VMEM((nclip, shard, width), bf16),
            dma((2, 2, ncap)), dma((2, ncap)),
            dma((2, nclip)), dma((2, nclip)),
            dma((ITERS + 1, ncap)), dma((ITERS + 1, ncap)),
            dma((ITERS, nclip)), dma((ITERS, nclip)),
            dma((ncap,)), dma((ncap,)),
            dma((nclip,)), dma((nclip,)),
        ],
        compiler_params=pltpu.CompilerParams(
            collective_id=0, has_side_effects=True, vmem_limit_bytes=66 * 1000 * 1000),
    )(teacher_audio, teacher_text, student_audio, student_text)


def solution(mesh):
    nclip, ncap = mesh.shape["clip"], mesh.shape["cap"]
    placed = (
        P(("clip", "cap"), None),
        P(("cap", "clip"), None),
        P(("clip", "cap"), None),
        P(("cap", "clip"), None),
    )
    return jax.shard_map(
        functools.partial(body, nclip, ncap),
        mesh=mesh,
        in_specs=placed,
        out_specs=(P(("clip", "cap"), None), P(("cap", "clip"), None)),
        check_vma=False,
    )
```

time: 284 us -> 86.3 us (0.30)
  blocking collectives: 115 us -> 0 us
  waiting for transfers between devices: 94 us -> 0 us
  Pallas kernels: 0 us -> 82.2 us
  matrix products: 52.1 us -> 0 us
  between operations: 13.9 us -> 0.65 us
  other arithmetic: 8.21 us -> 0 us
    pallas_call x0 -> x1, Pallas kernels: none -> 82.2 us  [body(): pl.pallas_call(functools.partial(kernel, nclip, ncap, shard), out_shape=(...]
    reduce_scatter x2 -> x0, waiting for transfers between devices: 80 us -> none  [the longest x1 48.7 us: body(): lax.psum_scatter(10.0 * contract_first(residual, audio_student), 'clip',...]
    psum x6 -> x0, blocking collectives: 63.7 us -> none  [the longest x3 36.4 us: body(): lax.psum(jnp.dot(weights_row, kernel, precision=lax.Precision.HIGHEST), '...]
    dot_general x10 -> x0, matrix products: 52.1 us -> none  [the longest x3 20.8 us: body(): jnp.dot(kernel, column_scale, precision=lax.Precision.HIGHEST)]
    all_gather x2 -> x0, blocking collectives: 39.4 us -> none  [the longest x1 21.5 us: body(): lax.all_gather(student_audio, 'cap', axis=0, tiled=True)]
    all_gather x2 -> x0, waiting for transfers between devices: 12.6 us -> none  [the longest x1 12.6 us: body(): lax.all_gather(student_text, 'clip', axis=0, tiled=True)]
    pmax x1 -> x0, blocking collectives: 11.8 us -> none  [body(): lax.pmax((jnp.max(teacher_logits, axis=1), jnp.max(student_logits, axis=1...]
    convert_element_type x1 -> x0, other arithmetic: 4.95 us -> none  [body(): residual = (student_prob - target).astype(jnp.bfloat16)]
  transfers between devices with their start and end apart: 4 -> 0, of which waited for: 3 -> 0; matrix products, arithmetic and copies ran while one was open for 3% -> 0% of each run, Pallas kernels for 0% -> 0%
where the time goes in v1:
time: 86.3 us; the launch traced here: 85.4 us
  Pallas kernels  82.2 us (95%)
  local copies, waits for them, and re-layouts  2.57 us (3%)
    pallas_call x1, Pallas kernels, body(): pl.pallas_call(functools.partial(kernel, nclip, ncap, shard), out_shape=(...  82.2 us
    unnamed x4, local copies, waits for them, and re-layouts  2.57 us

profile of v1, /device:TPU:0, one launch (start us, length us, event | category | flops | bytes accessed | tf_op | source)
XLA Modules:
  0.0 85.4 jit_solution(7138443249467068205)
XLA Ops:
  0.6 82.2 %shard_map.59 = (f32[192,512]{1,0:T(8,128)}, f32[192,512]{1,0:T(8,128)}) custom-call(bf16[192,512]{1,0:T(8,128)(2,1)} %ta_ref.1, bf16[192,512]{1,0:T(8,128)(2,1)} %tt_ref.1, bf16[192,512]{1,0:T(8,128)(2,1)} %sa_ref.1, bf16[192,512]{1,0:T(8,128)(2,1)} %st_ref.1), custom_call_target="tpu_custom_call" | custom-call | tf_op jit(solution)/shard_map/pallas_call | solution.py:442
  82.9 0.0 copy-start
  82.9 1.8 %copy.8 = f32[192,512]{1,0:T(8,128)} copy(f32[192,512]{1,0:T(8,128)} %get-tuple-element.4) | data formatting | bytes 786432
  84.7 0.0 copy-done
  84.7 0.7 copy.9
Async XLA Ops:
  82.9 1.8 %copy-start = (f32[192,512]{1,0:T(8,128)S(1)}, f32[192,512]{1,0:T(8,128)}, u32[]{:S(2)}) copy-start(f32[192,512]{1,0:T(8,128)} %get-tuple-element.5) | copy-start | bytes 1179652

commit v2 on v1

--- a/solution.py
+++ b/solution.py
@@ -59,9 +59,9 @@
     nclip, ncap, shard,
     ta_ref, tt_ref, sa_ref, st_ref, ag_ref, tg_ref,
     abuf, tbuf, kmat, smat, rmat, lbuf, pbuf, wrep, srep, crep, mrep, smax, ssum,
-    rowx, colx, maxx, lastx, asend, arecv, tsend, trecv,
+    rowx, colx, maxx, lastx, akeep, asend, arecv, tkeep, psend, precv, tsend, trecv,
     az_send, az_recv, tx_send, tx_recv, rx_send, rx_recv, cx_send, cx_recv,
-    as_send, as_recv, ts_send, ts_recv,
+    as_send, as_recv, ps_send, ps_recv, ts_send, ts_recv,
 ):
     clip = lax.axis_index("clip")
     cap = lax.axis_index("cap")
@@ -347,9 +347,16 @@
         wrep[...] = down(factor / total)
 
     text_student = tbuf.at[1].reshape(cols, width)
-
-    def audio_part(i, carry):
-        s = lax.rem(cap + 1 + i, ncap)
+    half_rows = shard // 2
+
+    def line_sum_copy(s, h, slot, step):
+        return remote(asend.at[s, h], arecv.at[slot, h], as_send.at[s, h], as_recv.at[slot, h], clip, cap + step)
+
+    def landed(slot, h):
+        here = arecv.at[slot, h]
+        remote(here, here, as_send.at[0, h], as_recv.at[slot, h], clip, cap).wait_recv()
+
+    def audio_part(s):
         rs = pl.ds(pl.multiple_of(s * shard, shard), shard)
         w, p = wrep[rs, :], srep[rs, :]
         for t in range(tiles):
@@ -357,44 +364,110 @@
             target = (w * kmat[rs, cs]) * crep[0:1, cs]
             rmat[rs, cs] = (smat[rs, cs].astype(jnp.float32) * p - target).astype(jnp.bfloat16)
         grad = 10.0 * jnp.dot(rmat[rs, :], text_student[...], preferred_element_type=jnp.float32)
-
-        @pl.when(i < ncap - 1)
-        def _():
-            asend[s] = grad.astype(jnp.bfloat16)
-            remote(asend.at[s], arecv.at[i + 1], as_send.at[i + 1], as_recv.at[i + 1], clip, s).start()
-
-        @pl.when(i == ncap - 1)
-        def _():
-            ag_ref[...] = grad
+        for h in range(2):
+            akeep[s, h] = grad[h * half_rows:(h + 1) * half_rows, :]
+
+    def first_send(s, slot, step):
+        for h in range(2):
+            asend[s, h] = akeep[s, h].astype(jnp.bfloat16)
+            line_sum_copy(s, h, slot, step).start()
+
+    def left_slot(s, d):
+        return s + (ncap - s) * (1 // d)
+
+    def audio_parts(i, carry):
+        d = ncap - 1 - i
+
+        @pl.when(cap + d < ncap)
+        def _():
+            s = cap + d
+            audio_part(s)
+
+            @pl.when(cap == 0)
+            def _():
+                first_send(s, s, 1)
+
+        @pl.when(cap >= d)
+        def _():
+            s = cap - d
+            audio_part(s)
+
+            @pl.when(cap == ncap - 1)
+            def _():
+                first_send(s, left_slot(s, d), -1)
         return carry
 
-    lax.fori_loop(0, ncap, audio_part, 0)
-
-    group = 2 if nclip % 2 == 0 else nclip
-    groups = nclip // group
+    lax.fori_loop(0, ncap - 1, audio_parts, 0)
+    audio_part(cap)
+
+    def relay_one(s, h, slot, step):
+        landed(s, h)
+        asend[s, h] = (akeep[s, h] + arecv[s, h].astype(jnp.float32)).astype(jnp.bfloat16)
+        line_sum_copy(s, h, slot, step).start()
+
+    def relay(d):
+        for h in range(2):
+            @pl.when(jnp.logical_and(cap >= 1, cap + d < ncap))
+            def _():
+                relay_one(cap + d, h, cap + d, 1)
+
+            @pl.when(jnp.logical_and(cap + 1 < ncap, cap >= d))
+            def _():
+                s = cap - d
+                relay_one(s, h, left_slot(s, d), -1)
+
+    groups = nclip // 2
+    chip, parity = clip // 2, clip % 2
     audio_student = abuf.at[1].reshape(rows, width)
 
-    def text_part(i, carry):
-        q = lax.rem(clip // group + 1 + i, groups)
-        cs = pl.ds(pl.multiple_of(q * (group * shard), LANE), group * shard)
-        grad = 10.0 * lax.dot_general(
-            rmat[:, cs], audio_student[...], (((0,), (0,)), ((), ())),
-            preferred_element_type=jnp.float32)
-        for g in range(group):
-            dest = q * group + g
-
-            @pl.when(dest == clip)
-            def _():
-                tg_ref[...] = grad[g * shard:(g + 1) * shard, :]
-
-            @pl.when(dest != clip)
-            def _():
-                offset = lax.rem(dest - clip + nclip, nclip)
-                tsend[dest] = grad[g * shard:(g + 1) * shard, :].astype(jnp.bfloat16)
-                remote(tsend.at[dest], trecv.at[offset], ts_send.at[offset], ts_recv.at[offset], dest, cap).start()
+    def pair_copy(q):
+        return remote(psend.at[q], precv.at[q], ps_send.at[q], ps_recv.at[q], flip(clip, 1), cap)
+
+    def text_copy(q, offset):
+        return remote(tsend.at[q], trecv.at[offset], ts_send.at[offset], ts_recv.at[offset], q * 2 + parity, cap)
+
+    def text_step(i, carry):
+        @pl.when(i < groups)
+        def _():
+            q = (chip + 1 + i) % groups
+            cs = pl.ds(pl.multiple_of(q * (2 * shard), LANE), 2 * shard)
+            grad = 10.0 * lax.dot_general(
+                rmat[:, cs], audio_student[...], (((0,), (0,)), ((), ())),
+                preferred_element_type=jnp.float32)
+            for g in range(2):
+                @pl.when(parity == g)
+                def _():
+                    psend[q] = grad[(1 - g) * shard:(2 - g) * shard, :].astype(jnp.bfloat16)
+                    tkeep[q] = grad[g * shard:(g + 1) * shard, :]
+            pair_copy(q).start()
+
+        @pl.when(i >= 1)
+        def _():
+            q = (chip + i) % groups
+            pair_copy(q).wait_recv()
+            both = tkeep[q] + precv[q].astype(jnp.float32)
+
+            @pl.when(i < groups)
+            def _():
+                tsend[q] = both.astype(jnp.bfloat16)
+                text_copy(q, i).start()
+
+            @pl.when(i == groups)
+            def _():
+                tg_ref[...] = both
         return carry
 
-    lax.fori_loop(0, groups, text_part, 0)
+    middle = max(groups // 2, 1)
+    lax.fori_loop(0, middle, text_step, 0)
+
+    def relays(i, carry):
+        relay(ncap - 2 - i)
+        return carry
+
+    lax.fori_loop(0, ncap - 3, relays, 0)
+    lax.fori_loop(middle, groups + 1, text_step, 0)
+    if ncap > 2:
+        relay(1)
 
     for t in range(2):
         for mask in range(1, nclip):
@@ -415,22 +488,41 @@
             return carry
         lax.fori_loop(0, ncap, drain, 0)
 
-    for j in range(1, ncap):
-        copy = remote(asend.at[0], arecv.at[j], as_send.at[j], as_recv.at[j], clip, cap)
+    def drain_sums(s, carry):
+        @pl.when(s != cap)
+        def _():
+            for h in range(2):
+                line_sum_copy(s, h, s, 0).wait_send()
+        return carry
+    lax.fori_loop(0, ncap, drain_sums, 0)
+
+    def drain_pairs(q, carry):
+        pair_copy(q).wait_send()
+        return carry
+    lax.fori_loop(0, groups, drain_pairs, 0)
+
+    total = tg_ref[...]
+    for j in range(1, groups):
+        copy = text_copy(chip, j)
         copy.wait_recv()
         copy.wait_send()
-    total = ag_ref[...]
-    for j in range(1, ncap):
-        total = total + arecv[j].astype(jnp.float32)
-    ag_ref[...] = total
-    for j in range(1, nclip):
-        copy = remote(tsend.at[0], trecv.at[j], ts_send.at[j], ts_recv.at[j], clip, cap)
-        copy.wait_recv()
-        copy.wait_send()
-    total = tg_ref[...]
-    for j in range(1, nclip):
         total = total + trecv[j].astype(jnp.float32)
     tg_ref[...] = total
+
+    for h in range(2):
+        ag_ref[h * half_rows:(h + 1) * half_rows, :] = akeep[cap, h]
+
+        def add(slot, h=h):
+            landed(slot, h)
+            ag_ref[h * half_rows:(h + 1) * half_rows, :] += arecv[slot, h].astype(jnp.float32)
+
+        @pl.when(cap >= 1)
+        def _():
+            add(cap)
+
+        @pl.when(cap + 1 < ncap)
+        def _():
+            add(ncap)
 
 
 def body(nclip, ncap, teacher_audio, teacher_text, student_audio, student_text):
@@ -462,16 +554,21 @@
             pltpu.VMEM((ITERS, nclip, 1, cols), f32),
             pltpu.VMEM((ncap, 1, rows), f32),
             pltpu.VMEM((ncap, 3, rows), f32),
-            pltpu.VMEM((ncap, shard, width), bf16),
-            pltpu.VMEM((ncap, shard, width), bf16),
-            pltpu.VMEM((nclip, shard, width), bf16),
-            pltpu.VMEM((nclip, shard, width), bf16),
+            pltpu.VMEM((ncap, 2, shard // 2, width), f32),
+            pltpu.VMEM((ncap, 2, shard // 2, width), bf16),
+            pltpu.VMEM((ncap + 1, 2, shard // 2, width), bf16),
+            pltpu.VMEM((nclip // 2, shard, width), f32),
+            pltpu.VMEM((nclip // 2, shard, width), bf16),
+            pltpu.VMEM((nclip // 2, shard, width), bf16),
+            pltpu.VMEM((nclip // 2, shard, width), bf16),
+            pltpu.VMEM((nclip // 2, shard, width), bf16),
             dma((2, 2, ncap)), dma((2, ncap)),
             dma((2, nclip)), dma((2, nclip)),
             dma((ITERS + 1, ncap)), dma((ITERS + 1, ncap)),
             dma((ITERS, nclip)), dma((ITERS, nclip)),
-            dma((ncap,)), dma((ncap,)),
-            dma((nclip,)), dma((nclip,)),
+            dma((ncap, 2)), dma((ncap + 1, 2)),
+            dma((nclip // 2,)), dma((nclip // 2,)),
+            dma((nclip // 2,)), dma((nclip // 2,)),
         ],
         compiler_params=pltpu.CompilerParams(
             collective_id=0, has_side_effects=True, vmem_limit_bytes=66 * 1000 * 1000),

time: 86.3 us -> 82.1 us (0.951)
  Pallas kernels: 82.2 us -> 78.7 us
    pallas_call x1, Pallas kernels: 82.2 us -> 78.7 us  [body(): pl.pallas_call(functools.partial(kernel, nclip, ncap, shard), out_shape=(...]
where the time goes in v2:
time: 82.1 us; the launch traced here: 81.9 us
  Pallas kernels  78.7 us (96%)
  local copies, waits for them, and re-layouts  2.57 us (3%)
    pallas_call x1, Pallas kernels, body(): pl.pallas_call(functools.partial(kernel, nclip, ncap, shard), out_shape=(...  78.7 us
    unnamed x4, local copies, waits for them, and re-layouts  2.57 us

profile of v2, /device:TPU:0, one launch (start us, length us, event | category | flops | bytes accessed | tf_op | source)
XLA Modules:
  0.0 81.9 jit_solution(17123127670780963496)
XLA Ops:
  0.6 78.7 %shard_map.59 = (f32[192,512]{1,0:T(8,128)}, f32[192,512]{1,0:T(8,128)}) custom-call(bf16[192,512]{1,0:T(8,128)(2,1)} %ta_ref.1, bf16[192,512]{1,0:T(8,128)(2,1)} %tt_ref.1, bf16[192,512]{1,0:T(8,128)(2,1)} %sa_ref.1, bf16[192,512]{1,0:T(8,128)(2,1)} %st_ref.1), custom_call_target="tpu_custom_call" | custom-call | tf_op jit(solution)/shard_map/pallas_call | solution.py:534
  79.3 0.0 copy-start
  79.3 1.8 %copy.8 = f32[192,512]{1,0:T(8,128)} copy(f32[192,512]{1,0:T(8,128)} %get-tuple-element.4) | data formatting | bytes 786432
  81.2 0.0 copy-done
  81.2 0.7 copy.9
Async XLA Ops:
  79.3 1.8 %copy-start = (f32[192,512]{1,0:T(8,128)S(1)}, f32[192,512]{1,0:T(8,128)}, u32[]{:S(2)}) copy-start(f32[192,512]{1,0:T(8,128)} %get-tuple-element.5) | copy-start | bytes 1179652

commit v3 on v2

--- a/solution.py
+++ b/solution.py
@@ -103,44 +103,48 @@
         landed = tbuf.at[t, flip_mask(clip, mask, nclip)]
         remote(landed, landed, tx_send.at[t, mask], tx_recv.at[t, mask], clip, cap).wait_recv()
 
-    def line_copy(t, s, step, own):
-        src = own_audio[t] if own else abuf.at[t, s]
+    def line_copy(t, s, h, step, own):
+        part = pl.ds(h * (shard // 2), shard // 2)
+        dst = abuf.at[t, s, part, :]
+        src = own_audio[t].at[part, :] if own else dst
         side = 0 if step < 0 else 1
-        return remote(src, abuf.at[t, s], az_send.at[t, side, s], az_recv.at[t, s], clip, cap + step)
+        return remote(src, dst, az_send.at[t, side, s, h], az_recv.at[t, s, h], clip, cap + step)
 
     def line_own(t):
+        for h in range(2):
+            @pl.when(cap + 1 < ncap)
+            def _():
+                line_copy(t, cap, h, 1, True).start()
+
+            @pl.when(cap >= 1)
+            def _():
+                line_copy(t, cap, h, -1, True).start()
+
+    def line_left(t, d, h):
+        s = cap - d
+        line_copy(t, s, h, 1, False).wait_recv()
+
         @pl.when(cap + 1 < ncap)
         def _():
-            line_copy(t, cap, 1, True).start()
+            line_copy(t, s, h, 1, False).start()
+
+    def line_right(t, d, h):
+        s = cap + d
+        line_copy(t, s, h, -1, False).wait_recv()
 
         @pl.when(cap >= 1)
         def _():
-            line_copy(t, cap, -1, True).start()
-
-    def line_left(t, d):
-        s = cap - d
-        line_copy(t, s, 1, False).wait_recv()
-
-        @pl.when(cap + 1 < ncap)
-        def _():
-            line_copy(t, s, 1, False).start()
-
-    def line_right(t, d):
-        s = cap + d
-        line_copy(t, s, -1, False).wait_recv()
-
-        @pl.when(cap >= 1)
-        def _():
-            line_copy(t, s, -1, False).start()
+            line_copy(t, s, h, -1, False).start()
 
     def line_step(t, d):
-        @pl.when(cap >= d)
-        def _():
-            line_left(t, d)
-
-        @pl.when(cap + d < ncap)
-        def _():
-            line_right(t, d)
+        for h in range(2):
+            @pl.when(cap >= d)
+            def _():
+                line_left(t, d, h)
+
+            @pl.when(cap + d < ncap)
+            def _():
+                line_right(t, d, h)
 
     step_cols = 512 if cols % 512 == 0 else LANE
 
@@ -175,17 +179,14 @@
     tree_forward(0, 0)
     line_own(0)
     sequence = mask_sequence(nclip, orders[0])
-    waited = 0
-    for d in range(1, ncap - 1):
-        amount = len(sequence) if d == ncap - 2 else min(len(sequence), waited + nclip // 2)
-        if d == 1:
-            line_step(0, 1)
-        for mask in sequence[waited:amount]:
-            tree_wait(0, mask)
-            tree_forward(0, mask)
-        waited = amount
-        if d > 1:
-            line_step(0, d)
+    waited = len(orders[0])
+    if ncap > 2:
+        line_step(0, 1)
+    for mask in sequence[:waited]:
+        tree_wait(0, mask)
+        tree_forward(0, mask)
+    for d in range(2, ncap - 1):
+        line_step(0, d)
     for mask in sequence[waited:]:
         tree_wait(0, mask)
         tree_forward(0, mask)
@@ -480,11 +481,13 @@
         def drain(s, carry, t=t):
             @pl.when(jnp.logical_and(s <= cap, cap + 1 < ncap))
             def _():
-                line_copy(t, s, 1, False).wait_send()
+                for h in range(2):
+                    line_copy(t, s, h, 1, False).wait_send()
 
             @pl.when(jnp.logical_and(s >= cap, cap >= 1))
             def _():
-                line_copy(t, s, -1, False).wait_send()
+                for h in range(2):
+                    line_copy(t, s, h, -1, False).wait_send()
             return carry
         lax.fori_loop(0, ncap, drain, 0)
 
@@ -562,7 +565,7 @@
             pltpu.VMEM((nclip // 2, shard, width), bf16),
             pltpu.VMEM((nclip // 2, shard, width), bf16),
             pltpu.VMEM((nclip // 2, shard, width), bf16),
-            dma((2, 2, ncap)), dma((2, ncap)),
+            dma((2, 2, ncap, 2)), dma((2, ncap, 2)),
             dma((2, nclip)), dma((2, nclip)),
             dma((ITERS + 1, ncap)), dma((ITERS + 1, ncap)),
             dma((ITERS, nclip)), dma((ITERS, nclip)),

time: 82.1 us -> 80.9 us (0.985)
  Pallas kernels: 78.7 us -> 77.5 us
    pallas_call x1, Pallas kernels: 78.7 us -> 77.5 us  [body(): pl.pallas_call(functools.partial(kernel, nclip, ncap, shard), out_shape=(...]
where the time goes in v3:
time: 80.9 us; the launch traced here: 80.7 us
  Pallas kernels  77.5 us (96%)
  local copies, waits for them, and re-layouts  2.57 us (3%)
    pallas_call x1, Pallas kernels, body(): pl.pallas_call(functools.partial(kernel, nclip, ncap, shard), out_shape=(...  77.5 us
    unnamed x4, local copies, waits for them, and re-layouts  2.57 us

profile of v3, /device:TPU:0, one launch (start us, length us, event | category | flops | bytes accessed | tf_op | source)
XLA Modules:
  0.0 80.7 jit_solution(10057209876471875252)
XLA Ops:
  0.6 77.5 %shard_map.59 = (f32[192,512]{1,0:T(8,128)}, f32[192,512]{1,0:T(8,128)}) custom-call(bf16[192,512]{1,0:T(8,128)(2,1)} %ta_ref.1, bf16[192,512]{1,0:T(8,128)(2,1)} %tt_ref.1, bf16[192,512]{1,0:T(8,128)(2,1)} %sa_ref.1, bf16[192,512]{1,0:T(8,128)(2,1)} %st_ref.1), custom_call_target="tpu_custom_call" | custom-call | tf_op jit(solution)/shard_map/pallas_call | solution.py:537
  78.2 0.0 copy-start
  78.2 1.8 %copy.8 = f32[192,512]{1,0:T(8,128)} copy(f32[192,512]{1,0:T(8,128)} %get-tuple-element.4) | data formatting | bytes 786432
  80.0 0.0 copy-done
  80.0 0.7 copy.9
Async XLA Ops:
  78.2 1.8 %copy-start = (f32[192,512]{1,0:T(8,128)S(1)}, f32[192,512]{1,0:T(8,128)}, u32[]{:S(2)}) copy-start(f32[192,512]{1,0:T(8,128)} %get-tuple-element.5) | copy-start | bytes 1179652

commit v4 on v3

--- a/solution.py
+++ b/solution.py
@@ -57,7 +57,7 @@
 
 def kernel(
     nclip, ncap, shard,
-    ta_ref, tt_ref, sa_ref, st_ref, ag_ref, tg_ref,
+    ta_ref, tt_ref, sa_ref, st_ref, out_ref,
     abuf, tbuf, kmat, smat, rmat, lbuf, pbuf, wrep, srep, crep, mrep, smax, ssum,
     rowx, colx, maxx, lastx, akeep, asend, arecv, tkeep, psend, precv, tsend, trecv,
     az_send, az_recv, tx_send, tx_recv, rx_send, rx_recv, cx_send, cx_recv,
@@ -67,6 +67,7 @@
     cap = lax.axis_index("cap")
     rows, cols, width = shard * ncap, shard * nclip, ta_ref.shape[1]
     tiles = cols // LANE
+    ag_ref, tg_ref = out_ref.at[0], out_ref.at[1]
     orders = tree_orders(nclip)
     if smat.shape != kmat.shape:
         smat = rmat
@@ -233,7 +234,6 @@
         for j in range(1, count):
             copy = remote(buffer.at[0], buffer.at[j], sends.at[k, j], recvs.at[k, j], clip, cap)
             copy.wait_recv()
-            copy.wait_send()
 
     def across(ref):
         return ref[...].T[0:1, :]
@@ -364,7 +364,7 @@
             cs = slice(t * LANE, (t + 1) * LANE)
             target = (w * kmat[rs, cs]) * crep[0:1, cs]
             rmat[rs, cs] = (smat[rs, cs].astype(jnp.float32) * p - target).astype(jnp.bfloat16)
-        grad = 10.0 * jnp.dot(rmat[rs, :], text_student[...], preferred_element_type=jnp.float32)
+        grad = jnp.dot(rmat[rs, :], text_student[...], preferred_element_type=jnp.float32)
         for h in range(2):
             akeep[s, h] = grad[h * half_rows:(h + 1) * half_rows, :]
 
@@ -432,7 +432,7 @@
         def _():
             q = (chip + 1 + i) % groups
             cs = pl.ds(pl.multiple_of(q * (2 * shard), LANE), 2 * shard)
-            grad = 10.0 * lax.dot_general(
+            grad = lax.dot_general(
                 rmat[:, cs], audio_student[...], (((0,), (0,)), ((), ())),
                 preferred_element_type=jnp.float32)
             for g in range(2):
@@ -470,6 +470,13 @@
     if ncap > 2:
         relay(1)
 
+    for k in range(ITERS + 1):
+        buffer = maxx if k == 0 else lastx if k == ITERS else rowx.at[k - 1]
+        for j in range(1, ncap):
+            remote(buffer.at[0], buffer.at[j], rx_send.at[k, j], rx_recv.at[k, j], clip, cap).wait_send()
+    for k in range(ITERS):
+        for j in range(1, nclip):
+            remote(colx.at[k, 0], colx.at[k, j], cx_send.at[k, j], cx_recv.at[k, j], clip, cap).wait_send()
     for t in range(2):
         for mask in range(1, nclip):
             bit = mask & -mask
@@ -534,11 +541,11 @@
     f32, bf16 = jnp.float32, jnp.bfloat16
     roomy = rows * cols <= 2 ** 21
     dma = pltpu.SemaphoreType.DMA
-    return pl.pallas_call(
+    grads = pl.pallas_call(
         functools.partial(kernel, nclip, ncap, shard),
-        out_shape=(jax.ShapeDtypeStruct((shard, width), f32),) * 2,
+        out_shape=jax.ShapeDtypeStruct((2, shard, width), f32),
         in_specs=[pl.BlockSpec(memory_space=pltpu.VMEM)] * 4,
-        out_specs=(pl.BlockSpec(memory_space=pltpu.VMEM),) * 2,
+        out_specs=pl.BlockSpec(memory_space=pltpu.VMEM),
         scratch_shapes=[
             pltpu.VMEM((2, ncap, shard, width), bf16),
             pltpu.VMEM((2, nclip, shard, width), bf16),
@@ -576,6 +583,7 @@
         compiler_params=pltpu.CompilerParams(
             collective_id=0, has_side_effects=True, vmem_limit_bytes=66 * 1000 * 1000),
     )(teacher_audio, teacher_text, student_audio, student_text)
+    return 10.0 * grads[0], 10.0 * grads[1]
 
 
 def solution(mesh):

time: 80.9 us -> 80.3 us (level)
  local copies, waits for them, and re-layouts: 2.57 us -> 0 us
  other arithmetic: 0 us -> 2.06 us
    unnamed x4 -> x0, local copies, waits for them, and re-layouts: 2.57 us -> none
    mul x0 -> x1, other arithmetic: none -> 2.06 us  [body(): return (10.0 * grads[0], 10.0 * grads[1])]
where the time goes in v4:
time: 80.3 us; the launch traced here: 80.2 us
  Pallas kernels  77.5 us (97%)
  other arithmetic  2.06 us (3%)
    pallas_call x1, Pallas kernels, body(): pl.pallas_call(functools.partial(kernel, nclip, ncap, shard), out_shape=j...  77.5 us
    mul x1, other arithmetic, body(): return (10.0 * grads[0], 10.0 * grads[1])  2.06 us

profile of v4, /device:TPU:0, one launch (start us, length us, event | category | flops | bytes accessed | tf_op | source)
XLA Modules:
  0.0 80.2 jit_solution(8575583588837253230)
XLA Ops:
  0.6 77.5 %shard_map.59 = f32[2,192,512]{2,1,0:T(8,128)} custom-call(bf16[192,512]{1,0:T(8,128)(2,1)} %ta_ref.1, bf16[192,512]{1,0:T(8,128)(2,1)} %tt_ref.1, bf16[192,512]{1,0:T(8,128)(2,1)} %sa_ref.1, bf16[192,512]{1,0:T(8,128)(2,1)} %st_ref.1), custom_call_target="tpu_custom_call" | custom-call | tf_op jit(solution)/shard_map/pallas_call | solution.py:544
  78.1 2.1 %multiply_bitcast_fusion = (f32[192,512]{1,0:T(8,128)}, f32[192,512]{1,0:T(8,128)}) fusion(f32[2,192,512]{2,1,0:T(8,128)} %shard_map.59), kind=kLoop, calls=%fused_computation | loop fusion | flops 196608 | bytes 1572864 | tf_op jit(solution)/shard_map/mul | solution.py:586
